TPU v7x, 512 devices: a whole 4x4x16 slice. The times are simulated.
512 devices in a mesh: dp: 2 (over core), ctx: 32 (over x, z_lo), tensor: 8 (over z_hi, y).
Axes of the slice: x: 4, y: 4, z: 16 (z_hi: 2, z_lo: 8; z = z_hi * 8 + z_lo), core: 2. Of those that a mesh axis runs over, the one named last changes fastest.
Arguments:
- tokens: bfloat16 [2, 4096, 2048], P('dp', 'ctx', 'tensor'), may hold values from -6 to 6
- cotangent: bfloat16 [2, 4096, 2048], P('dp', 'ctx', 'tensor'), may hold values from -6 to 6
- w_value: bfloat16 [2048, 2048], P('ctx', 'tensor'), may hold values from -0.125 to 0.125
- w_gate: bfloat16 [2048, 2048], P('ctx', 'tensor'), may hold values from -0.125 to 0.125
- decay_rate: float32 [4, 2048], P(None, 'tensor'), as said below
- residue: float32 [4, 2048], P(None, 'tensor'), may hold values from -4 to 4
- skip_gain: float32 [2048], P('tensor'), may hold values from -4 to 4
- contig_len: int32 [2, 8], P('dp'), may hold values from 1 to 1536, 4096 in all within a row
Outputs:
- output: bfloat16 [2, 4096, 2048], P('dp', 'ctx', 'tensor')
- grad_tokens: bfloat16 [2, 4096, 2048], P('dp', 'ctx', 'tensor')
- grad_w_value: float32 [2048, 2048], P('ctx', 'tensor')
- grad_w_gate: float32 [2048, 2048], P('ctx', 'tensor')
- grad_skip: float32 [2048], P('tensor')
- grad_residue: float32 [4, 2048], P(None, 'tensor')
- grad_rate: float32 [4, 2048], P(None, 'tensor')
Inputs may be any that keep to these rules, and one draw needn't show every extreme that they name: `contig_len`: each row's lengths sum to 4096; the largest of each row is exactly 1536. `decay_rate`: every rate lies between 0.25 / 4096 and 1 / 30.
All inputs are finite; a program needn't handle non-finite values.
Results may differ from a plain program's by a relative error of at most 0.012.
Values may be sent and summed in bfloat16 or wider, within the bound.
A program may use at most 64 MiB of HBM per device.

v0:
```python
import jax
import jax.numpy as jnp
from jax import lax
from jax.sharding import PartitionSpec as P


def carried_in(part, axis, combine, identity, reverse):
    count = lax.axis_size(axis)
    place = lax.axis_index(axis)
    ahead = count - 1 - place if reverse else place
    gathered = jax.tree.map(lambda a: lax.all_gather(a, axis), part)
    state = jax.tree.map(lambda a, e: jnp.zeros_like(a) + jnp.asarray(e, a.dtype), part, identity)

    def one(hop, state):
        source = count - 1 - hop if reverse else hop
        return combine(
            state, jax.tree.map(lambda a: lax.dynamic_index_in_dim(a, source, 0, False), gathered)
        )

    return lax.fori_loop(0, ahead, one, state)


def link(first, second):
    return (first[0] * second[0], second[0] * first[1] + second[1])


def body(tokens, cotangent, w_value, w_gate, decay_rate, residue, skip_gain, contig_len):
    rows, span, width = tokens.shape
    flat = tokens.reshape(rows * span, width)
    feats = lax.all_gather(flat, "tensor", axis=1, tiled=True)
    paired_w = jnp.concatenate([w_value, w_gate], axis=1)
    whole = lax.all_gather(paired_w, "ctx", axis=0, tiled=True)
    both = jnp.dot(feats, whole, preferred_element_type=jnp.float32)
    value = both[:, :width].reshape(rows, span, width)
    gate = both[:, width:].reshape(rows, span, width)
    me = lax.axis_index("ctx")
    first = me * span
    positions = first + jnp.arange(span, dtype=jnp.int32)
    starts = jnp.cumsum(contig_len, axis=1) - contig_len
    here = starts[:, None, :]
    place = positions[None, :, None]
    reset = jnp.any(place == here, axis=2).astype(jnp.float32)
    reset_next = jnp.any(place + 1 == here, axis=2).astype(jnp.float32)
    clear_fwd = jnp.all((here < first) | (here > place), axis=2).astype(jnp.float32)
    clear_back = jnp.all((here <= place) | (here > first + span), axis=2).astype(jnp.float32)
    pole = jnp.exp(-decay_rate)
    factor = jnp.sqrt(-jnp.expm1(-2.0 * decay_rate))
    weight_mode = residue * factor
    steps_in = (jnp.arange(span, dtype=jnp.int32) + 1).astype(jnp.float32)
    decay_fwd = jnp.exp(-decay_rate[None] * steps_in[:, None, None])
    decay_back = decay_fwd[::-1]
    keep = (1.0 - reset)[:, :, None, None] * pole
    drive = jnp.broadcast_to(value[:, :, None, :], keep.shape)
    local = lax.associative_scan(link, (keep, drive), axis=1)[1]
    scale_end = decay_fwd[-1][None] * clear_fwd[:, -1][:, None, None]
    end_state = local[:, -1]
    _, incoming = carried_in(
        (scale_end, end_state),
        "ctx",
        link,
        (jnp.ones_like(scale_end), jnp.zeros_like(end_state)),
        False,
    )
    state = local + decay_fwd[None] * clear_fwd[:, :, None, None] * incoming[:, None]
    mixed = jnp.sum(weight_mode * state, axis=2) + skip_gain * value
    output = (gate * mixed).astype(jnp.bfloat16)
    upstream = cotangent.astype(jnp.float32)
    grad_mixed = upstream * gate
    grad_gate = upstream * mixed
    keep_back = (1.0 - reset_next)[:, :, None, None] * pole
    source = grad_mixed[:, :, None, :] * weight_mode
    local_back = lax.associative_scan(link, (keep_back[:, ::-1], source[:, ::-1]), axis=1)[1][
        :, ::-1
    ]
    scale_top = decay_back[0][None] * clear_back[:, 0][:, None, None]
    top_state = local_back[:, 0]
    _, incoming_back = carried_in(
        (scale_top, top_state),
        "ctx",
        link,
        (jnp.ones_like(scale_top), jnp.zeros_like(top_state)),
        True,
    )
    grad_state = (
        local_back + decay_back[None] * clear_back[:, :, None, None] * incoming_back[:, None]
    )
    grad_value = jnp.sum(grad_state, axis=2) + skip_gain * grad_mixed
    skip_part = jnp.sum(grad_mixed * value, axis=(0, 1))
    paired_part = jnp.sum(grad_mixed[:, :, None, :] * state, axis=(0, 1))
    carried_part = jnp.sum(grad_state * (state - drive), axis=(0, 1))
    grad_skip, paired, carried = lax.psum((skip_part, paired_part, carried_part), ("dp", "ctx"))
    grad_residue = factor * paired
    grad_rate = -carried + residue * jnp.exp(-2.0 * decay_rate) / factor * paired
    cot_both = (
        jnp.concatenate([grad_value, grad_gate], axis=2)
        .astype(jnp.bfloat16)
        .reshape(rows * span, 2 * width)
    )
    contract = (((1,), (1,)), ((), ()))
    term = lax.dot_general(cot_both, whole, contract, preferred_element_type=jnp.float32)
    grad_tokens = lax.psum_scatter(
        term.astype(jnp.bfloat16), "tensor", scatter_dimension=1, tiled=True
    )
    grad_tokens = grad_tokens.reshape(rows, span, width)
    slabs = lax.all_to_all(feats, "ctx", split_axis=1, concat_axis=0, tiled=True)
    grad_w = lax.dot_general(
        slabs,
        lax.all_gather(cot_both, "ctx", axis=0, tiled=True),
        (((0,), (0,)), ((), ())),
        preferred_element_type=jnp.float32,
    )
    grad_w = lax.psum(grad_w, "dp")
    return (
        output,
        grad_tokens,
        grad_w[:, :width],
        grad_w[:, width:],
        grad_skip,
        grad_residue,
        grad_rate,
    )


def solution(mesh):
    in_specs = (
        P("dp", "ctx", "tensor"),
        P("dp", "ctx", "tensor"),
        P("ctx", "tensor"),
        P("ctx", "tensor"),
        P(None, "tensor"),
        P(None, "tensor"),
        P("tensor"),
        P("dp", None),
    )
    out_specs = (
        P("dp", "ctx", "tensor"),
        P("dp", "ctx", "tensor"),
        P("ctx", "tensor"),
        P("ctx", "tensor"),
        P("tensor"),
        P(None, "tensor"),
        P(None, "tensor"),
    )
    return jax.shard_map(body, mesh=mesh, in_specs=in_specs, out_specs=out_specs, check_vma=False)
```

profile of v0, /device:TPU:17, one launch (start us, length us, event | category | flops | bytes accessed | tf_op | source)
XLA Modules:
  0.0 1120.3 jit_solution(10773666285794444207)
XLA Ops:
  7.2 1.4 pad_maximum_fusion.5
  8.7 0.8 reduce_window_sum.11
  12.6 1.0 copy.23
  13.6 0.7 fusion.29
  14.7 0.7 slice.435
  16.0 117.6 %all-gather.2 = f32[32,4,256]{2,1,0:T(4,128)} all-gather(f32[1,4,256]{2,1,0:T(4,128)S(1)} %get-tuple-element.204), channel_id=4, replica_groups=mesh['dp'=2,'ctx'=32,'tensor'=8] {'ctx'}, dimensions={0}, use_global_device_ids=true | all-gather | bytes 135168 | tf_op jit(solution)/shard_map/all_gather | solution.py:11
  133.6 104.2 %all-gather.1 = f32[32,4,256]{2,1,0:T(4,128)} all-gather(f32[1,4,256]{2,1,0:T(4,128)S(1)} %get-tuple-element.205), channel_id=3, replica_groups=mesh['dp'=2,'ctx'=32,'tensor'=8] {'ctx'}, dimensions={0}, use_global_device_ids=true | all-gather | bytes 135168 | tf_op jit(solution)/shard_map/all_gather | solution.py:11
  237.8 53.8 %all-gather = bf16[1,128,2048]{1,2,0:T(8,128)(2,1)S(1)} all-gather(bf16[1,128,256]{1,2,0:T(8,128)(2,1)S(1)} %copy.23), channel_id=2, replica_groups=mesh['dp'=2,'ctx'=32,'tensor'=8] {'tensor'}, dimensions={2}, use_global_device_ids=true | all-gather | bytes 589824 | tf_op jit(solution)/shard_map/all_gather | solution.py:30
  291.7 2.1 convolution_bitcast_fusion
  296.5 0.8 slice.489
  298.9 0.7 pad_maximum_fusion.7
  301.4 0.8 pad.112
  302.2 0.8 pad.113
  303.8 1.0 slice_multiply_fusion
  306.9 0.7 pad_maximum_fusion.10
  307.8 0.7 pad_maximum_fusion.8
  308.7 0.7 pad_maximum_fusion.6
  309.9 0.7 fusion.9
  310.6 101.0 %all_gather.34 = f32[32,1,4,256]{3,2,1,0:T(4,128)S(1)} all-gather(f32[1,1,4,256]{3,2,1,0:T(4,128)} %slice_add_fusion.10), channel_id=1, replica_groups=mesh['dp'=2,'ctx'=32,'tensor'=8] {'ctx'}, dimensions={0}, use_global_device_ids=true | all-gather | bytes 135168 | tf_op jit(solution)/shard_map/all_gather | solution.py:11
  411.6 21.3 %while.27 = (s32[]{:T(128)}, f32[1,4,256]{2,1,0:T(4,128)S(1)}, s32[]{:T(128)}, f32[32,1,4,256]{3,2,1,0:T(4,128)}, f32[32,1,4,256]{3,2,1,0:T(4,128)S(1)}, /*index=5*/s32[]{:T(128)}, s32[]{:T(128)}, s32[]{:T(128)}, s32[]{:T(128)}) while((s32[]{:T(128)}, f32[1,4,256]{2,1,0:T(4,128)S(1)}, s32[]{:T(128)}, f32[32,1,4,256]{3,2,1,0:T(4,128)}, ...), condition=%wide.region_9.10_spmd, body=%wide.region_8.9_spmd.sunk | while | flops 2054 | bytes 16535 | solution.py:20
  411.6 0.7 bitcast_add_fusion.7
  412.3 0.7 bitcast_add_fusion.7
  413.7 0.7 bitcast_add_fusion.7
  414.4 0.7 bitcast_add_fusion.7
  415.1 0.7 bitcast_add_fusion.7
  415.8 0.7 bitcast_add_fusion.7
  416.5 0.7 bitcast_add_fusion.7
  417.1 0.7 bitcast_add_fusion.7
  417.8 0.7 bitcast_add_fusion.7
  418.5 0.7 bitcast_add_fusion.7
  419.2 0.7 bitcast_add_fusion.7
  419.9 0.7 bitcast_add_fusion.7
  420.6 0.7 bitcast_add_fusion.7
  421.3 0.7 bitcast_add_fusion.7
  421.9 0.7 bitcast_add_fusion.7
  422.6 0.7 bitcast_add_fusion.7
  423.3 0.7 bitcast_add_fusion.7
  424.0 0.7 bitcast_add_fusion.7
  424.7 0.7 bitcast_add_fusion.7
  425.4 0.7 bitcast_add_fusion.7
  426.1 0.7 bitcast_add_fusion.7
  426.8 0.7 bitcast_add_fusion.7
  427.5 0.7 bitcast_add_fusion.7
  428.1 0.7 bitcast_add_fusion.7
  428.8 0.7 bitcast_add_fusion.7
  429.5 0.7 bitcast_add_fusion.7
  430.2 0.7 bitcast_add_fusion.7
  430.9 0.7 bitcast_add_fusion.7
  431.6 0.7 bitcast_add_fusion.7
  432.3 0.7 bitcast_add_fusion.7
  433.0 0.9 pad_maximum_fusion.2
  434.7 0.8 add.297
  435.5 1.0 fusion.4
  436.5 0.7 broadcast_in_dim.10
  437.2 0.8 pad.98
  438.1 22.1 %pad.99 = f32[1,128,4,256]{3,2,1,0:T(4,128)S(1)} pad(f32[1,64,4,256]{3,2,1,0:T(4,128)} %add.297, f32[]{:T(128)} %constant.69.clone.1), padding=0_0_0x1_0_1x0_0_0x0_0_0 | pad | bytes 786436 | tf_op jit(solution)/shard_map/pad | solution.py:54
  460.2 98.4 %all_gather.31 = f32[32,1,4,256]{3,2,1,0:T(4,128)S(1)} all-gather(f32[1,1,4,256]{3,2,1,0:T(4,128)S(1)} %slice_add_fusion.12), channel_id=1, replica_groups=mesh['dp'=2,'ctx'=32,'tensor'=8] {'ctx'}, dimensions={0}, use_global_device_ids=true | all-gather | bytes 135168 | tf_op jit(solution)/shard_map/all_gather | solution.py:11
  558.6 2.3 multiply_reduce_fusion
  561.8 44.6 %all_to_all.19 = bf16[128,32,64]{0,2,1:T(8,128)(2,1)S(1)} all-to-all(bf16[128,32,64]{0,2,1:T(8,128)(2,1)S(1)} %bitcast.93), channel_id=1, replica_groups=mesh['dp'=2,'ctx'=32,'tensor'=8] {'ctx'}, dimensions={1} | all-to-all | bytes 1048576 | tf_op jit(solution)/shard_map/all_to_all | solution.py:105
  606.4 246.9 %all-gather.8.cloned.1.call-done = bf16[4096,512]{1,0:T(8,128)(2,1)} async-done(((bf16[128,512]{1,0:T(8,128)(2,1)}), bf16[4096,512]{1,0:T(8,128)(2,1)}) %all-gather.8.cloned.1.call-update) | async-done | bytes 4194320 | tf_op jit(solution)/shard_map/all_gather | solution.py:108
  853.3 3.7 convolution_bitcast_fusion.1
  857.1 1.6 convolution_convert_fusion
  858.7 252.3 %all-reduce.28 = (f32[256]{0:T(256)}, f32[4,256]{1,0:T(4,128)S(1)}, f32[4,256]{1,0:T(4,128)S(1)}) all-reduce(f32[256]{0:T(256)S(1)} %get-tuple-element.210, f32[4,256]{1,0:T(4,128)S(1)} %get-tuple-element.169, f32[4,256]{1,0:T(4,128)S(1)} %get-tuple-element.167), channel_id=1, replica_groups=mesh['dp'=2,'ctx'=32,'tensor'=8] {'dp','ctx'}, use_global_device_ids=true, to_apply=%region_14.15 | all-reduce | flops 2304 | bytes 18432 | tf_op jit(solution)/shard_map/psum | solution.py:91
  1112.3 1.5 fusion.33
  (139 shorter events, 16.7 us)
Async XLA Ops:
  7.2 284.6 %all-gather.6.cloned.1.call-start = ((), (), s32[]{:S(2)}) async-start(), calls=%async_computation.2 | async-start | bytes 2162688 | tf_op jit(solution)/shard_map/all_gather | solution.py:32
  8.6 844.6 %all-gather.8.cloned.1.call-start = ((), (), s32[]{:S(2)}) async-start(), calls=%async_computation.4 | async-start | bytes 4325376 | tf_op jit(solution)/shard_map/all_gather | solution.py:108
  15.4 0.6 copy-start.10
  291.7 4.7 copy-start.5
  296.4 0.9 copy-start.2
  296.5 1.7 copy-start
  298.6 2.5 copy-start.3
  298.6 2.5 copy-start.4
  300.0 1.3 slice-start
  434.7 123.9 %copy-start.11 = (f32[128]{0:T(128)S(1)}, f32[128]{0:T(128)}, u32[]{:S(2)}) copy-start(f32[128]{0:T(128)} %copy-done.10) | copy-start | bytes 1540
  438.1 122.9 %copy-start.6 = (bf16[1,128,256]{2,1,0:T(8,128)(2,1)S(1)}, bf16[1,128,256]{2,1,0:T(8,128)(2,1)}, u32[]{:S(2)}) copy-start(bf16[1,128,256]{2,1,0:T(8,128)(2,1)} %param.13) | copy-start | bytes 196612
  438.1 122.9 %copy-start.9 = (f32[256]{0:T(256)S(1)}, f32[256]{0:T(256)}, u32[]{:S(2)}) copy-start(f32[256]{0:T(256)} %param.18) | copy-start | bytes 3076
  561.7 550.6 %all-reduce.31.cloned.1.call-start = ((), (), s32[]{:S(2)}) async-start(), calls=%async_computation.5 | async-start | bytes 262144 | tf_op jit(solution)/shard_map/psum | solution.py:112
  606.4 250.7 %copy-start.1 = (bf16[2048,512]{1,0:T(8,128)(2,1)S(1)}, bf16[2048,512]{1,0:T(8,128)(2,1)}, u32[]{:S(2)}) copy-start(bf16[2048,512]{1,0:T(8,128)(2,1)} %all-gather.6.cloned.1.call-done) | copy-start | bytes 6291460
  857.0 254.0 %copy-start.7 = (f32[4,256]{1,0:T(4,128)S(1)}, f32[4,256]{1,0:T(4,128)}, u32[]{:S(2)}) copy-start(f32[4,256]{1,0:T(4,128)} %param.17) | copy-start | bytes 12292
  857.0 254.0 %copy-start.8 = (f32[4,256]{1,0:T(4,128)S(1)}, f32[4,256]{1,0:T(4,128)}, u32[]{:S(2)}) copy-start(f32[4,256]{1,0:T(4,128)} %param.16) | copy-start | bytes 12292
  857.0 256.8 %reduce-scatter.2.cloned.1.call-start = ((), (), s32[]{:S(2)}) async-start(), calls=%async_computation.3 | async-start | bytes 589824 | tf_op jit(solution)/shard_map/reduce_scatter | solution.py:101
Sparse Core Ops, SparseCore 0:
  10.6 209.9 all-gather.5
  561.8 291.4 all-gather.7
  857.1 59.6 all-reduce.30
  921.7 110.2 reduce-scatter.1
where the time goes:
time: 1120 us
  blocking collectives  772 us (69%)
  waiting for transfers between devices  247 us (22%)
  other arithmetic  40.2 us (4%)
  local copies, waits for them, and re-layouts  38.6 us (3%)
  between operations  15 us (1%)
    all_gather x4, blocking collectives, carried_in(): gathered = jax.tree.map(lambda a: lax.all_gather(a, axis), part)  421 us
    psum x1, blocking collectives, body(): lax.psum((skip_part, paired_part, carried_part), ('dp', 'ctx'))  252 us
    all_gather x1, waiting for transfers between devices, body(): lax.all_gather(cot_both, 'ctx', axis=0, tiled=True)  247 us
    all_gather x1, blocking collectives, body(): feats = lax.all_gather(flat, 'tensor', axis=1, tiled=True)  53.8 us
    all_to_all x1, blocking collectives, body(): lax.all_to_all(feats, 'ctx', split_axis=1, concat_axis=0, tiled=True)  44.6 us
    pad x12, local copies, waits for them, and re-layouts, body(): local = lax.associative_scan(link, (keep, drive), axis=1)[1]  24.6 us
    add x42, other arithmetic, link(): return (first[0] * second[0], second[0] * first[1] + second[1])  23.3 us
  transfers between devices with their start and end apart: 4, of which 1 were waited for; matrix products, arithmetic and copies ran while one was open for 1% of the time, Pallas kernels for 0%

commit v1 on v0

--- a/solution.py
+++ b/solution.py
@@ -88,7 +88,9 @@
     skip_part = jnp.sum(grad_mixed * value, axis=(0, 1))
     paired_part = jnp.sum(grad_mixed[:, :, None, :] * state, axis=(0, 1))
     carried_part = jnp.sum(grad_state * (state - drive), axis=(0, 1))
-    grad_skip, paired, carried = lax.psum((skip_part, paired_part, carried_part), ("dp", "ctx"))
+    grad_skip, paired, carried = lax.psum(
+        lax.psum((skip_part, paired_part, carried_part), axis_name="dp"), axis_name="ctx"
+    )
     grad_residue = factor * paired
     grad_rate = -carried + residue * jnp.exp(-2.0 * decay_rate) / factor * paired
     cot_both = (

time: 1120 us -> 1040 us (0.929)
  the two profiles are of different devices: /device:TPU:17 before, /device:TPU:2 now
where the time goes in v1:
time: 1040 us
  blocking collectives  708 us (68%)
  waiting for transfers between devices  231 us (22%)
  other arithmetic  40.3 us (4%)
  local copies, waits for them, and re-layouts  38.5 us (4%)
  between operations  15 us (1%)
    all_gather x4, blocking collectives, carried_in(): gathered = jax.tree.map(lambda a: lax.all_gather(a, axis), part)  450 us
    all_gather x1, waiting for transfers between devices, body(): lax.all_gather(cot_both, 'ctx', axis=0, tiled=True)  180 us
    psum x1, blocking collectives, body(): lax.psum(lax.psum((skip_part, paired_part, carried_part), axis_name='dp')...  115 us
    all_to_all x1, blocking collectives, body(): lax.all_to_all(feats, 'ctx', split_axis=1, concat_axis=0, tiled=True)  75.8 us
    all_gather x1, blocking collectives, body(): feats = lax.all_gather(flat, 'tensor', axis=1, tiled=True)  64.8 us
    reduce_scatter x1, waiting for transfers between devices, body(): lax.psum_scatter(term.astype(jnp.bfloat16), 'tensor', scatter_dimension=1...  51.1 us
    pad x12, local copies, waits for them, and re-layouts, body(): local = lax.associative_scan(link, (keep, drive), axis=1)[1]  24.6 us
    add x42, other arithmetic, link(): return (first[0] * second[0], second[0] * first[1] + second[1])  23.3 us
  transfers between devices with their start and end apart: 4, of which 2 were waited for; matrix products, arithmetic and copies ran while one was open for 1% of the time, Pallas kernels for 0%

profile of v1, /device:TPU:2, one launch (start us, length us, event | category | flops | bytes accessed | tf_op | source)
XLA Modules:
  0.0 1040.9 jit_solution(18058453001255904874)
XLA Ops:
  7.2 1.4 pad_maximum_fusion.5
  8.7 0.8 reduce_window_sum.11
  12.7 1.0 copy.23
  13.7 0.7 fusion.29
  14.8 0.7 slice.435
  16.1 119.5 %all-gather.2 = f32[32,4,256]{2,1,0:T(4,128)} all-gather(f32[1,4,256]{2,1,0:T(4,128)S(1)} %get-tuple-element.207), channel_id=4, replica_groups=mesh['dp'=2,'ctx'=32,'tensor'=8] {'ctx'}, dimensions={0}, use_global_device_ids=true | all-gather | bytes 135168 | tf_op jit(solution)/shard_map/all_gather | solution.py:11
  135.6 107.9 %all-gather.1 = f32[32,4,256]{2,1,0:T(4,128)} all-gather(f32[1,4,256]{2,1,0:T(4,128)S(1)} %get-tuple-element.208), channel_id=3, replica_groups=mesh['dp'=2,'ctx'=32,'tensor'=8] {'ctx'}, dimensions={0}, use_global_device_ids=true | all-gather | bytes 135168 | tf_op jit(solution)/shard_map/all_gather | solution.py:11
  243.5 64.8 %all-gather = bf16[1,128,2048]{1,2,0:T(8,128)(2,1)S(1)} all-gather(bf16[1,128,256]{1,2,0:T(8,128)(2,1)S(1)} %copy.23), channel_id=2, replica_groups=mesh['dp'=2,'ctx'=32,'tensor'=8] {'tensor'}, dimensions={2}, use_global_device_ids=true | all-gather | bytes 589824 | tf_op jit(solution)/shard_map/all_gather | solution.py:30
  308.3 2.1 convolution_bitcast_fusion
  313.1 0.8 slice.489
  315.5 0.7 pad_maximum_fusion.7
  318.0 0.8 pad.112
  318.8 0.8 pad.113
  320.4 1.0 slice_multiply_fusion
  323.5 0.7 pad_maximum_fusion.10
  324.4 0.7 pad_maximum_fusion.8
  325.3 0.7 pad_maximum_fusion.6
  326.5 0.7 fusion.9
  327.2 105.8 %all_gather.34 = f32[32,1,4,256]{3,2,1,0:T(4,128)S(1)} all-gather(f32[1,1,4,256]{3,2,1,0:T(4,128)} %slice_add_fusion.10), channel_id=1, replica_groups=mesh['dp'=2,'ctx'=32,'tensor'=8] {'ctx'}, dimensions={0}, use_global_device_ids=true | all-gather | bytes 135168 | tf_op jit(solution)/shard_map/all_gather | solution.py:11
  433.1 15.8 %while.27 = (s32[]{:T(128)}, f32[1,4,256]{2,1,0:T(4,128)S(1)}, s32[]{:T(128)}, f32[32,1,4,256]{3,2,1,0:T(4,128)}, f32[32,1,4,256]{3,2,1,0:T(4,128)S(1)}, /*index=5*/s32[]{:T(128)}, s32[]{:T(128)}, s32[]{:T(128)}, s32[]{:T(128)}) while((s32[]{:T(128)}, f32[1,4,256]{2,1,0:T(4,128)S(1)}, s32[]{:T(128)}, f32[32,1,4,256]{3,2,1,0:T(4,128)}, ...), condition=%wide.region_9.10_spmd, body=%wide.region_8.9_spmd.sunk | while | flops 2054 | bytes 16535 | solution.py:20
  433.1 0.7 bitcast_add_fusion.7
  433.8 0.7 bitcast_add_fusion.7
  434.4 0.7 bitcast_add_fusion.7
  435.1 0.7 bitcast_add_fusion.7
  435.8 0.7 bitcast_add_fusion.7
  436.5 0.7 bitcast_add_fusion.7
  437.9 0.7 bitcast_add_fusion.7
  438.6 0.7 bitcast_add_fusion.7
  439.3 0.7 bitcast_add_fusion.7
  439.9 0.7 bitcast_add_fusion.7
  440.6 0.7 bitcast_add_fusion.7
  441.3 0.7 bitcast_add_fusion.7
  442.0 0.7 bitcast_add_fusion.7
  442.7 0.7 bitcast_add_fusion.7
  443.4 0.7 bitcast_add_fusion.7
  444.1 0.7 bitcast_add_fusion.7
  445.5 0.7 bitcast_add_fusion.7
  446.2 0.7 bitcast_add_fusion.7
  446.8 0.7 bitcast_add_fusion.7
  447.5 0.7 bitcast_add_fusion.7
  448.2 0.7 bitcast_add_fusion.7
  448.9 0.9 pad_maximum_fusion.2
  450.7 0.8 add.303
  451.4 1.0 fusion.4
  452.4 0.7 broadcast_in_dim.10
  453.1 0.8 pad.98
  454.0 22.1 %pad.99 = f32[1,128,4,256]{3,2,1,0:T(4,128)S(1)} pad(f32[1,64,4,256]{3,2,1,0:T(4,128)} %add.303, f32[]{:T(128)} %constant.69.clone.1), padding=0_0_0x1_0_1x0_0_0x0_0_0 | pad | bytes 786436 | tf_op jit(solution)/shard_map/pad | solution.py:54
  476.1 117.2 %all_gather.31 = f32[32,1,4,256]{3,2,1,0:T(4,128)S(1)} all-gather(f32[1,1,4,256]{3,2,1,0:T(4,128)S(1)} %slice_add_fusion.12), channel_id=1, replica_groups=mesh['dp'=2,'ctx'=32,'tensor'=8] {'ctx'}, dimensions={0}, use_global_device_ids=true | all-gather | bytes 135168 | tf_op jit(solution)/shard_map/all_gather | solution.py:11
  593.3 5.5 while.26
  593.3 0.7 bitcast_add_fusion.6
  594.7 0.7 bitcast_add_fusion.6
  595.3 0.7 bitcast_add_fusion.6
  596.0 0.7 bitcast_add_fusion.6
  597.4 0.7 bitcast_add_fusion.6
  598.1 0.7 bitcast_add_fusion.6
  598.8 2.3 multiply_reduce_fusion
  601.9 75.8 %all_to_all.19 = bf16[128,32,64]{0,2,1:T(8,128)(2,1)S(1)} all-to-all(bf16[128,32,64]{0,2,1:T(8,128)(2,1)S(1)} %bitcast.93), channel_id=1, replica_groups=mesh['dp'=2,'ctx'=32,'tensor'=8] {'ctx'}, dimensions={1} | all-to-all | bytes 1048576 | tf_op jit(solution)/shard_map/all_to_all | solution.py:107
  677.7 180.3 %all-gather.8.cloned.1.call-done = bf16[4096,512]{1,0:T(8,128)(2,1)} async-done(((bf16[128,512]{1,0:T(8,128)(2,1)}), bf16[4096,512]{1,0:T(8,128)(2,1)}) %all-gather.8.cloned.1.call-update) | async-done | bytes 4194320 | tf_op jit(solution)/shard_map/all_gather | solution.py:110
  858.0 3.7 convolution_bitcast_fusion.1
  861.7 1.6 convolution_convert_fusion
  863.4 2.5 all-reduce.29
  865.9 114.6 %all-reduce.28 = (f32[256]{0:T(256)}, f32[4,256]{1,0:T(4,128)S(1)}, f32[4,256]{1,0:T(4,128)S(1)}) all-reduce(f32[256]{0:T(256)S(1)} %get-tuple-element.198, f32[4,256]{1,0:T(4,128)S(1)} %get-tuple-element.199, f32[4,256]{1,0:T(4,128)S(1)} %get-tuple-element.200), channel_id=1, replica_groups=mesh['dp'=2,'ctx'=32,'tensor'=8] {'ctx'}, use_global_device_ids=true, to_apply=%region_15.16 | all-reduce | flops 2304 | bytes 18432 | tf_op jit(solution)/shard_map/psum | solution.py:91
  981.8 1.5 fusion.33
  983.3 51.1 %reduce-scatter.2.cloned.1.call-done = bf16[128,256]{1,0:T(8,128)(2,1)} async-done(((bf16[128,2048]{1,0:T(8,128)(2,1)}), bf16[128,256]{1,0:T(8,128)(2,1)}) %reduce-scatter.2.cloned.1.call-update) | async-done | bytes 65552 | tf_op jit(solution)/shard_map/reduce_scatter | solution.py:103
  (140 shorter events, 18.8 us)
Async XLA Ops:
  7.2 301.2 %all-gather.6.cloned.1.call-start = ((), (), s32[]{:S(2)}) async-start(), calls=%async_computation.2 | async-start | bytes 2162688 | tf_op jit(solution)/shard_map/all_gather | solution.py:32
  8.6 849.3 %all-gather.8.cloned.1.call-start = ((), (), s32[]{:S(2)}) async-start(), calls=%async_computation.4 | async-start | bytes 4325376 | tf_op jit(solution)/shard_map/all_gather | solution.py:110
  15.5 0.5 copy-start.10
  308.3 4.7 copy-start.5
  313.0 0.9 copy-start.2
  313.1 1.7 copy-start
  315.2 2.5 copy-start.3
  315.2 2.5 copy-start.4
  316.6 1.3 slice-start
  450.7 148.1 %copy-start.11 = (f32[128]{0:T(128)S(1)}, f32[128]{0:T(128)}, u32[]{:S(2)}) copy-start(f32[128]{0:T(128)} %copy-done.10) | copy-start | bytes 1540
  454.0 147.1 %copy-start.6 = (bf16[1,128,256]{2,1,0:T(8,128)(2,1)S(1)}, bf16[1,128,256]{2,1,0:T(8,128)(2,1)}, u32[]{:S(2)}) copy-start(bf16[1,128,256]{2,1,0:T(8,128)(2,1)} %param.13) | copy-start | bytes 196612
  454.0 147.1 %copy-start.9 = (f32[256]{0:T(256)S(1)}, f32[256]{0:T(256)}, u32[]{:S(2)}) copy-start(f32[256]{0:T(256)} %param.18) | copy-start | bytes 3076
  601.9 379.9 %all-reduce.32.cloned.1.call-start = ((), (), s32[]{:S(2)}) async-start(), calls=%async_computation.5 | async-start | bytes 262144 | tf_op jit(solution)/shard_map/psum | solution.py:114
  677.7 184.0 %copy-start.1 = (bf16[2048,512]{1,0:T(8,128)(2,1)S(1)}, bf16[2048,512]{1,0:T(8,128)(2,1)}, u32[]{:S(2)}) copy-start(bf16[2048,512]{1,0:T(8,128)(2,1)} %all-gather.6.cloned.1.call-done) | copy-start | bytes 6291460
  861.6 118.8 %copy-start.7 = (f32[4,256]{1,0:T(4,128)S(1)}, f32[4,256]{1,0:T(4,128)}, u32[]{:S(2)}) copy-start(f32[4,256]{1,0:T(4,128)} %param.17) | copy-start | bytes 12292
  861.6 118.8 %copy-start.8 = (f32[4,256]{1,0:T(4,128)S(1)}, f32[4,256]{1,0:T(4,128)}, u32[]{:S(2)}) copy-start(f32[4,256]{1,0:T(4,128)} %param.16) | copy-start | bytes 12292
  861.7 172.7 %reduce-scatter.2.cloned.1.call-start = ((), (), s32[]{:S(2)}) async-start(), calls=%async_computation.3 | async-start | bytes 589824 | tf_op jit(solution)/shard_map/reduce_scatter | solution.py:103
Sparse Core Ops, SparseCore 0:
  10.6 213.3 all-gather.5
  602.0 255.9 all-gather.7
  861.8 53.5 all-reduce.31
  920.3 113.9 reduce-scatter.1
